TPU v7x, 32 devices: a whole 2x2x4 slice. The times are simulated.
32 devices in a mesh: grp: 4 (over y, core), blk: 8 (over z, x).
Axes of the slice: x: 2, y: 2, z: 4, core: 2. Of those that a mesh axis runs over, the one named last changes fastest.
Arguments:
- unlabeled: bfloat16 [16384, 1024], P('blk'), may hold values from -10 to 10
- labeled: bfloat16 [32768, 1024], P(('grp', 'blk')), may hold values from -5 to 5
- picks: int32 [128], replicated, may hold values from 0 to 16383, as said below
Outputs:
- nearest: float32 [16384], P('blk')
Inputs may be any that keep to these rules, and one draw needn't show every extreme that they name: `picks`: indices may repeat; row 0 and row 16383 are always among them.
All inputs are finite; a program needn't handle non-finite values.
Results may differ from a plain program's by a relative error of at most 0.0003.
Values may be sent and summed in bfloat16 or wider, within the bound.
No kernel may reach another device: no remote copies, remote signals or barrier semaphores. Data moves between devices by JAX's collectives and lax.ppermute only.
A program may use at most 64 MiB of HBM per device.

v0:
```python
import jax
import jax.numpy as jnp
from jax import lax
from jax.sharding import PartitionSpec as P

STEPS = 2


def from_behind(block, axis, distance):
    devices = range(lax.axis_size(axis))
    route = [((i - distance) % len(devices), i) for i in devices]
    return lax.ppermute(block, axis, route)


def squares(rows):
    wide = rows.astype(jnp.float32)
    return jnp.sum(wide * wide, axis=1)


def least(rows, rows_sq, others, width):
    others_sq = squares(others)
    inner = lax.dot_general(
        rows, others, (((1,), (1,)), ((), ())), preferred_element_type=jnp.float32
    )
    scaled = (rows_sq[:, None] + others_sq[None, :] - 2.0 * inner) / width
    return jnp.min(scaled, axis=1)


def body(unlabeled, labeled, picks):
    width = unlabeled.shape[1]
    rows_dev = unlabeled.shape[0]
    rows_sq = squares(unlabeled)
    labeled_min = least(unlabeled, rows_sq, labeled, width)
    moving = labeled
    for step in range(STEPS):
        moving = from_behind(moving, "blk", 1)
        labeled_min = jnp.minimum(labeled_min, least(unlabeled, rows_sq, moving, width))
    offset = lax.axis_index("blk") * rows_dev
    local = picks - offset
    owned = (local >= 0) & (local < rows_dev)
    taken = unlabeled[jnp.clip(local, 0, rows_dev - 1)]
    chosen = jnp.where(owned[:, None], taken.astype(jnp.float32), 0.0)
    pick_rows = lax.psum(chosen.astype(jnp.bfloat16), "blk")
    pick_min = least(unlabeled, rows_sq, pick_rows, width)
    combined = jnp.minimum(labeled_min, pick_min)
    combined = lax.pmin(combined, "grp")
    return combined


def solution(mesh):
    return jax.shard_map(
        body,
        mesh=mesh,
        in_specs=(P("blk", None), P(("grp", "blk"), None), P()),
        out_specs=P("blk"),
        check_vma=False,
    )
```

profile of v0, /device:TPU:0, one launch (start us, length us, event | category | flops | bytes accessed | tf_op | source)
XLA Modules:
  0.0 184.7 jit_solution(11573937873616090945)
XLA Ops:
  6.5 0.0 all-reduce.2.cloned.1.call-start
  6.5 3.0 %collective-permute-start = (bf16[1024,1024]{1,0:T(8,128)(2,1)}, bf16[1024,1024]{1,0:T(8,128)(2,1)}, u32[]{:S(2)}, u32[]{:S(2)}) collective-permute-start(bf16[1024,1024]{1,0:T(8,128)(2,1)} %param.4), channel_id=1, source_target_pairs={{7,0},{0,1},{1,2},{2,3},{3,4},{4,5},{5,6},{6,7},{15,8},{8,9},{9,10... | collective-permute-start | bytes 6291464 | tf_op jit(solution)/shard_map/ppermute | solution.py:12
  9.5 0.7 compare_select_fusion
  10.2 3.8 %gather_fusion = bf16[128,1024]{1,0:T(8,128)(2,1)S(1)} fusion(bf16[2048,1024]{1,0:T(8,128)(2,1)} %param.3, s32[1024]{0:T(1024)S(1)} %pad_clamp_fusion), kind=kCustom, calls=%fused_computation | custom fusion | bytes 524800 | tf_op jit(solution)/shard_map/gather | solution.py:41
  14.0 0.7 compare_and_fusion
  14.6 0.8 select_convert_fusion
  15.4 0.0 all-reduce.2.cloned.1.call-update
  15.5 0.0 copy-done.2
  15.5 0.0 copy-start
  15.5 0.5 multiply_reduce_fusion.6
  16.0 3.3 %multiply_reduce_fusion.3 = f32[2048]{0:T(1024)S(1)} fusion(bf16[2048,1024]{1,0:T(8,128)(2,1)} %param.3), kind=kLoop, calls=%fused_computation.4 | loop fusion | flops 6289408 | bytes 4202496 | tf_op jit(solution)/shard_map/reduce_sum | solution.py:17
  19.3 42.2 %collective-permute-done = bf16[1024,1024]{1,0:T(8,128)(2,1)} collective-permute-done((bf16[1024,1024]{1,0:T(8,128)(2,1)}, bf16[1024,1024]{1,0:T(8,128)(2,1)}, u32[]{:S(2)}, u32[]{:S(2)}) %collective-permute-start) | collective-permute-done | bytes 2097184 | tf_op jit(solution)/shard_map/ppermute | solution.py:12
  61.5 0.0 collective-permute-start.1
  61.5 5.0 %multiply_reduce_fusion.2 = f32[2048]{0:T(1024)S(1)} fusion(bf16[2048,1024]{1,0:T(8,128)(2,1)S(1)} %copy-done, bf16[1024,1024]{1,0:T(8,128)(2,1)S(1)} %copy-done.2, f32[1024]{0:T(1024)S(1)} %multiply_reduce_fusion.6, f32[2048]{0:T(1024)S(1)} %multiply_reduce_fusion.3), kind=kOutput, calls=%fused_computation.3 | convolution fusion | flops 4305451008 | bytes 6311936 | tf_op jit(solution)/shard_map/dot_general | solution.py:22
  66.5 82.3 %all-reduce.2.cloned.1.call-done = bf16[128,1024]{1,0:T(8,128)(2,1)} async-done(((bf16[128,1024]{1,0:T(8,128)(2,1)}), bf16[128,1024]{1,0:T(8,128)(2,1)}) %all-reduce.2.cloned.1.call-update) | async-done | bytes 262160 | tf_op jit(solution)/shard_map/psum | solution.py:43
  148.9 1.2 multiply_reduce_fusion.7
  150.1 3.9 %fusion.3 = f32[2048]{0:T(1024)S(1)} fusion(bf16[128,1024]{1,0:T(8,128)(2,1)} %all-reduce.2.cloned.1.call-done, bf16[2048,1024]{1,0:T(8,128)(2,1)} %param.3, f32[128]{0:T(128)S(1)} %multiply_reduce_fusion.7, f32[2048]{0:T(1024)S(1)} %multiply_reduce_fusion.3), kind=kOutput, calls=%fused_computation.12 | convolution fusion | flops 538179584 | bytes 4473344 | tf_op jit(solution)/shard_map/dot_general | solution.py:22
  154.0 2.1 %multiply_reduce_fusion.5 = f32[1024]{0:T(1024)S(1)} fusion(bf16[1024,1024]{1,0:T(8,128)(2,1)} %collective-permute-done), kind=kLoop, calls=%fused_computation.6 | loop fusion | flops 3144704 | bytes 2101248 | tf_op jit(solution)/shard_map/reduce_sum | solution.py:17
  156.1 0.0 copy-done.1
  156.1 6.6 %multiply_reduce_fusion.1 = f32[2048]{0:T(1024)S(1)} fusion(bf16[2048,1024]{1,0:T(8,128)(2,1)S(1)} %copy-done.1, bf16[1024,1024]{1,0:T(8,128)(2,1)} %collective-permute-done, f32[1024]{0:T(1024)S(1)} %multiply_reduce_fusion.5, f32[2048]{0:T(1024)S(1)} %multiply_reduce_fusion.3), kind=kOutput, calls=%fused_computation.2 | convolution fusion | flops 4305451008 | bytes 6311936 | tf_op jit(solution)/shard_map/dot_general | solution.py:22
  162.7 0.0 collective-permute-done.1
  162.8 2.1 %multiply_reduce_fusion.4 = f32[1024]{0:T(1024)S(1)} fusion(bf16[1024,1024]{1,0:T(8,128)(2,1)} %collective-permute-done.1), kind=kLoop, calls=%fused_computation.5 | loop fusion | flops 3144704 | bytes 2101248 | tf_op jit(solution)/shard_map/reduce_sum | solution.py:17
  164.8 6.6 %multiply_reduce_fusion = f32[2048]{0:T(1024)S(1)} fusion(bf16[2048,1024]{1,0:T(8,128)(2,1)S(1)} %copy-done.1, bf16[1024,1024]{1,0:T(8,128)(2,1)} %collective-permute-done.1, f32[1024]{0:T(1024)S(1)} %multiply_reduce_fusion.4, f32[2048]{0:T(1024)S(1)} %multiply_reduce_fusion.3), kind=kOutput, calls=%fused_computation.1 | convolution fusion | flops 4305451008 | bytes 6311936 | tf_op jit(solution)/shard_map/dot_general | solution.py:22
  171.5 6.3 %pmin.7 = f32[2048]{0:T(1024)} all-reduce(f32[2048]{0:T(1024)S(1)} %minimum_minimum_fusion), channel_id=1, replica_groups=mesh['grp'=4,'blk'=8] {'grp'}, use_global_device_ids=true, to_apply=%region_10.11 | all-reduce | flops 2048 | bytes 16384 | tf_op jit(solution)/shard_map/pmin | solution.py:46
  (5 shorter events, 0.0 us)
Async XLA Ops:
  6.5 8.9 %copy-start.2 = (bf16[1024,1024]{1,0:T(8,128)(2,1)S(1)}, bf16[1024,1024]{1,0:T(8,128)(2,1)}, u32[]{:S(2)}) copy-start(bf16[1024,1024]{1,0:T(8,128)(2,1)} %param.4) | copy-start | bytes 6291460
  6.5 142.3 %all-reduce.2.cloned.1.call-start = ((), (), s32[]{:S(2)}) async-start(), calls=%async_computation | async-start | bytes 524288 | tf_op jit(solution)/shard_map/psum | solution.py:43
  6.5 54.9 %collective-permute-start = (bf16[1024,1024]{1,0:T(8,128)(2,1)}, bf16[1024,1024]{1,0:T(8,128)(2,1)}, u32[]{:S(2)}, u32[]{:S(2)}) collective-permute-start(bf16[1024,1024]{1,0:T(8,128)(2,1)} %param.4), channel_id=1, source_target_pairs={{7,0},{0,1},{1,2},{2,3},{3,4},{4,5},{5,6},{6,7},{15,8},{8,9},{9,10... | collective-permute-start | bytes 6291464 | tf_op jit(solution)/shard_map/ppermute | solution.py:12
  15.5 46.0 %copy-start = (bf16[2048,1024]{1,0:T(8,128)(2,1)S(1)}, bf16[2048,1024]{1,0:T(8,128)(2,1)}, u32[]{:S(2)}) copy-start(bf16[2048,1024]{1,0:T(8,128)(2,1)} %param.3) | copy-start | bytes 12582916
  61.5 101.3 %collective-permute-start.1 = (bf16[1024,1024]{1,0:T(8,128)(2,1)}, bf16[1024,1024]{1,0:T(8,128)(2,1)}, u32[]{:S(2)}, u32[]{:S(2)}) collective-permute-start(bf16[1024,1024]{1,0:T(8,128)(2,1)} %collective-permute-done), channel_id=1, source_target_pairs={{7,0},{0,1},{1,2},{2,3},{3,4},{4,5},{5,6},{6,7},{15,8},{8,9},{9,10... | collective-permute-start | bytes 6291464 | tf_op jit(solution)/shard_map/ppermute | solution.py:12
  148.9 7.2 %copy-start.1 = (bf16[2048,1024]{1,0:T(8,128)(2,1)S(1)}, bf16[2048,1024]{1,0:T(8,128)(2,1)}, u32[]{:S(2)}) copy-start(bf16[2048,1024]{1,0:T(8,128)(2,1)} %param.3) | copy-start | bytes 12582916
Sparse Core Ops, SparseCore 0:
  15.6 133.2 all-reduce.1
where the time goes:
time: 185 us
  waiting for transfers between devices  125 us (68%)
  matrix products  22.2 us (12%)
  between operations  13.5 us (7%)
  other arithmetic  11.3 us (6%)
  blocking collectives  6.35 us (3%)
  local copies, waits for them, and re-layouts  3.79 us (2%)
  starting transfers between devices  2.97 us (2%)
    psum x1, waiting for transfers between devices, body(): pick_rows = lax.psum(chosen.astype(jnp.bfloat16), 'blk')  82.3 us
    ppermute x2, waiting for transfers between devices, from_behind(): return lax.ppermute(block, axis, route)  42.2 us
    dot_general x4, matrix products, least(): lax.dot_general(rows, others, (((1,), (1,)), ((), ())), preferred_element...  22.2 us
    reduce_sum x5, other arithmetic, squares(): return jnp.sum(wide * wide, axis=1)  9.17 us
    pmin x1, blocking collectives, body(): combined = lax.pmin(combined, 'grp')  6.35 us
    gather x1, local copies, waits for them, and re-layouts, body(): taken = unlabeled[jnp.clip(local, 0, rows_dev - 1)]  3.77 us
  transfers between devices with their start and end apart: 3, of which 2 were waited for; matrix products, arithmetic and copies ran while one was open for 15% of the time, Pallas kernels for 0%

commit v1 on v0

v1 whole, which is shorter than its diff:
```python
import functools

import jax
import jax.numpy as jnp
from jax import lax
from jax.experimental import pallas as pl
from jax.experimental.pallas import tpu as pltpu
from jax.sharding import PartitionSpec as P


FORWARD = (144, 192)
BOTH = 2
AXES = ("grp", "blk")
TILE = 256
LANES = 128
PACK = 16
KERNEL_BYTES = 16 * 2**20


ANY = pl.BlockSpec(memory_space=pl.ANY)
VMEM = pl.BlockSpec(memory_space=pltpu.VMEM)
SMEM = pl.BlockSpec(memory_space=pltpu.SMEM)


def squares(rows):
    wide = rows.astype(jnp.float32)
    return jnp.sum(wide * wide, axis=1)


def aligned(at):
    return pl.multiple_of(at, PACK)


def cut_kernel(place, sizes, source, *refs):
    outs, sems = refs[:-1], refs[-1]
    copies = []
    for k, size in enumerate(sizes):
        rows = source.at[pl.ds(aligned(place(k)), size)]
        copies.append(pltpu.make_async_copy(rows, outs[k], sems.at[k]))
    for copy in copies:
        copy.start()
    for copy in copies:
        copy.wait()


def cut(source, place, sizes):
    width = source.shape[1]
    return pl.pallas_call(
        functools.partial(cut_kernel, place, sizes),
        out_shape=[jax.ShapeDtypeStruct((n, width), source.dtype) for n in sizes],
        in_specs=[ANY],
        out_specs=[VMEM] * len(sizes),
        scratch_shapes=[pltpu.SemaphoreType.DMA((len(sizes),))],
        cost_estimate=pl.CostEstimate(
            flops=0, bytes_accessed=4 * width * sum(sizes), transcendentals=0
        ),
        compiler_params=pltpu.CompilerParams(vmem_limit_bytes=KERNEL_BYTES),
    )(source)


def gather_kernel(share, picks, table, out, hold, pattern, sem):
    first = lax.axis_index("grp") * share
    base = lax.axis_index("blk") * table.shape[0]
    lane = lax.broadcasted_iota(jnp.int32, (1, share * PACK), 1)
    for p in range(share):
        local = picks[first + p] - base
        owned = (local >= 0) & (local < table.shape[0])
        row = jnp.clip(local, 0, table.shape[0] - 1)
        within = row & (PACK - 1)
        copy = pltpu.make_async_copy(
            table.at[pl.ds(aligned(row - within), PACK)],
            hold.at[pl.ds(p * PACK, PACK)],
            sem,
        )
        copy.start()
        spot = jnp.where(owned, p * PACK + within, -1)
        pattern[p : p + 1, :] = jnp.where(lane == spot, 1.0, 0.0)
    pltpu.make_async_copy(table.at[pl.ds(0, share * PACK)], hold, sem).wait()
    taken = jnp.dot(
        pattern[...].astype(hold.dtype), hold[...], preferred_element_type=jnp.float32
    )
    out[...] = taken.astype(out.dtype)


def gather(picks, table, share):
    width = table.shape[1]
    return pl.pallas_call(
        functools.partial(gather_kernel, share),
        out_shape=jax.ShapeDtypeStruct((share, width), table.dtype),
        in_specs=[SMEM, ANY],
        out_specs=VMEM,
        scratch_shapes=[
            pltpu.VMEM((share * PACK, width), table.dtype),
            pltpu.VMEM((share, share * PACK), jnp.float32),
            pltpu.SemaphoreType.DMA,
        ],
        cost_estimate=pl.CostEstimate(
            flops=2 * share * share * PACK * width,
            bytes_accessed=2 * share * PACK * width,
            transcendentals=0,
        ),
        compiler_params=pltpu.CompilerParams(vmem_limit_bytes=KERNEL_BYTES),
    )(picks, table)


def score_kernel(sizes, lead, picked, *refs):
    sources = refs[: len(sizes)]
    refs = list(refs[len(sizes) :])
    near, far, near_half, far_half = refs[:4]
    extra = refs[4:6] if picked else ()
    out, rows, beyond, best, sems = refs[-5:]
    copies = []
    at = 0
    for k, size in enumerate(sizes):
        copies.append(
            pltpu.make_async_copy(sources[k], rows.at[pl.ds(at, size)], sems.at[k])
        )
        at += size
    total, main = at, sum(sizes[:lead])
    other = pltpu.make_async_copy(far, beyond, sems.at[len(sizes)])
    for copy in copies:
        copy.start()
    other.start()
    best[...] = jnp.full_like(best, -jnp.inf)

    def against(block, halves, tile, count):
        for t in range(0, block.shape[0], tile):
            inner = lax.dot_general(
                rows[0:count, :],
                block[t : t + tile, :],
                (((1,), (1,)), ((), ())),
                preferred_element_type=jnp.float32,
            )
            gain = inner - halves[:, t : t + tile]
            reach = min(tile, LANES)
            top = gain[:, :reach]
            for k in range(LANES, tile, LANES):
                top = jnp.maximum(top, gain[:, k : k + LANES])
            best[0:count, 0:reach] = jnp.maximum(best[0:count, 0:reach], top)

    for copy in copies[:lead]:
        copy.wait()
    against(near, near_half, TILE, main)
    other.wait()
    against(beyond, far_half, TILE, main)
    for copy in copies[lead:]:
        copy.wait()
    if picked:
        against(extra[0], extra[1], extra[0].shape[0], total)
    out[...] = jnp.max(best[...].T, axis=0, keepdims=True)


def score(chunks, near, far, near_half, far_half, only=(), picked=()):
    sizes = [chunk.shape[0] for chunk in (*chunks, *only)]
    main = sum(chunk.shape[0] for chunk in chunks)
    total = sum(sizes)
    padded = -(-total // LANES) * LANES
    width = near.shape[1]
    block = near.shape[0]
    out = pl.pallas_call(
        functools.partial(score_kernel, sizes, len(chunks), bool(picked)),
        out_shape=jax.ShapeDtypeStruct((1, padded), jnp.float32),
        in_specs=[ANY] * len(sizes) + [VMEM, ANY, VMEM, VMEM] + [VMEM] * len(picked),
        out_specs=VMEM,
        scratch_shapes=[
            pltpu.VMEM((total, width), jnp.bfloat16),
            pltpu.VMEM((block, width), jnp.bfloat16),
            pltpu.VMEM((padded, LANES), jnp.float32),
            pltpu.SemaphoreType.DMA((len(sizes) + 1,)),
        ],
        cost_estimate=pl.CostEstimate(
            flops=4 * main * block * width,
            bytes_accessed=2 * width * (total + 2 * block),
            transcendentals=0,
        ),
        compiler_params=pltpu.CompilerParams(vmem_limit_bytes=KERNEL_BYTES),
    )(*chunks, *only, near, far, near_half, far_half, *picked)
    return out[0]


def body(n_grp, n_blk, unlabeled, labeled, picks):
    width = unlabeled.shape[1]
    rows_dev = unlabeled.shape[0]
    half = rows_dev // 2
    grp = lax.axis_index("grp")
    side, core = grp // 2, grp % 2
    odd = lax.axis_index("blk") % 2 == 1

    def send(value, move):
        pairs = []
        for g in range(n_grp):
            for b in range(n_blk):
                to_g, to_b = move(g, b)
                pairs.append((g * n_blk + b, to_g * n_blk + to_b))
        return lax.ppermute(value, AXES, pairs)

    back_two = lambda g, b: (g, (b - 2) % n_blk)
    ahead_two = lambda g, b: (g, (b + 2) % n_blk)
    ahead_one = lambda g, b: (g, (b + 1) % n_blk)
    swap_x = lambda g, b: (g, b ^ 1)
    swap_core = lambda g, b: (g ^ 1, b)
    swap_side = lambda g, b: (g ^ 2, b)
    swap_both = lambda g, b: (g ^ 3, b)

    edge = sum(FORWARD)
    middle = half - 2 * edge
    rest = [middle - middle // BOTH // PACK * PACK * (BOTH - 1)]
    rest += [middle // BOTH // PACK * PACK] * (BOTH - 1)

    def half_start():
        return (lax.axis_index("grp") % 2) * half

    def edge_start(k):
        far_side = lax.axis_index("grp") // 2
        return half_start() + far_side * (half - edge) + sum(FORWARD[:k])

    def rest_start(k):
        return half_start() + edge + sum(rest[:k])

    def far_edge():
        near_side = 1 - lax.axis_index("grp") // 2
        return half_start() + near_side * (half - edge)

    mine = list(cut(unlabeled, edge_start, list(FORWARD)))
    *between, beyond = cut(
        unlabeled, lambda k: rest_start(k) if k < BOTH else far_edge(), rest + [edge]
    )
    mine += between
    two = [send(chunk, back_two) for chunk in mine]
    far = send(labeled, swap_core)
    near_half = 0.5 * squares(labeled)
    far_half = send(near_half, swap_core)[None, :]
    near_half = near_half[None, :]

    def best(chunks, *more):
        return score(chunks, labeled, far, near_half, far_half, *more)

    def for_x(k):
        return jnp.where(odd, mine[k], two[k])

    one = [send(for_x(k), swap_x) for k in range(4)]
    two_side = [send(two[k], swap_side) for k in range(2)]
    one_side = [send(one[k], swap_side) for k in range(2)]

    own_a = best(mine)
    z_edge = best(two[:2])
    mid = best(two_side + two[2:] + one[:2])
    x_rest = best(one[2:] + one_side)

    chosen = gather(picks, unlabeled, picks.shape[0] // n_grp)
    hop = 1
    while hop < n_blk:
        chosen = chosen + send(chosen, lambda g, b: (g, b ^ hop))
        hop *= 2
    chosen = jnp.concatenate([chosen, send(chosen, swap_core)])
    chosen_half = 0.5 * squares(chosen)[None, :]
    own_b = best([beyond], mine, (chosen, chosen_half))

    def ordered(near, between, beyond):
        lower = jnp.where(side == 0, near, beyond)
        upper = jnp.where(side == 0, beyond, near)
        return jnp.concatenate([lower, between, upper])

    two_all = ordered(z_edge[:edge], mid[edge : edge + middle], mid[:edge])
    from_two = send(two_all, ahead_two)
    mid_later, _ = lax.optimization_barrier((mid, two_all))
    own_near = jnp.maximum(own_a[: edge + middle], own_b[edge:half])
    own_all = ordered(own_near[:edge], own_near[edge:], own_b[:edge])
    at = edge + middle
    one_all = ordered(
        mid_later[at : at + edge], x_rest[:middle], x_rest[middle : middle + edge]
    )
    from_one = send(one_all, ahead_one)
    rows_sq = squares(unlabeled)
    home = jnp.maximum(own_all, from_two)
    home = jnp.maximum(home, from_one)
    mine_best = jnp.maximum(home, send(home, swap_side))
    other_best = jnp.maximum(send(home, swap_core), send(home, swap_both))
    top = jnp.concatenate(
        [
            jnp.where(core == 0, mine_best, other_best),
            jnp.where(core == 0, other_best, mine_best),
        ]
    )
    return (rows_sq - 2.0 * top) / width


def solution(mesh):
    n_grp, n_blk = mesh.shape["grp"], mesh.shape["blk"]

    def run(unlabeled, labeled, picks):
        return body(n_grp, n_blk, unlabeled, labeled, picks)

    return jax.shard_map(
        run,
        mesh=mesh,
        in_specs=(P("blk", None), P(("grp", "blk"), None), P()),
        out_specs=P("blk"),
        check_vma=False,
    )
```

time: 185 us -> 120 us (0.65)
  waiting for transfers between devices: 125 us -> 47.7 us
  starting transfers between devices: 2.97 us -> 30.1 us
  Pallas kernels: 0 us -> 26.2 us
  matrix products: 22.2 us -> 0 us
  between operations: 13.5 us -> 0.26 us
  blocking collectives: 6.35 us -> 0 us
    psum x1 -> x0, waiting for transfers between devices: 82.3 us -> none  [body(): pick_rows = lax.psum(chosen.astype(jnp.bfloat16), 'blk')]
    ppermute x2 -> x23, starting transfers between devices: 2.97 us -> 30.1 us  [send(): return lax.ppermute(value, AXES, pairs)]
    pallas_call x0 -> x8, Pallas kernels: none -> 26.2 us  [the longest x5 22.8 us: score(): pl.pallas_call(functools.partial(score_kernel, sizes, len(chunks), bool(p...]
    dot_general x4 -> x0, matrix products: 22.2 us -> none  [least(): lax.dot_general(rows, others, (((1,), (1,)), ((), ())), preferred_element...]
    reduce_sum x5 -> x3, other arithmetic: 9.17 us -> 2.36 us  [squares(): return jnp.sum(wide * wide, axis=1)]
    pmin x1 -> x0, blocking collectives: 6.35 us -> none  [body(): combined = lax.pmin(combined, 'grp')]
    ppermute x2 -> x23, waiting for transfers between devices: 42.2 us -> 47.7 us  [send(): return lax.ppermute(value, AXES, pairs)]
    unnamed x6 -> x26, local copies, waits for them, and re-layouts: 0.01 us -> 5.09 us
  transfers between devices with their start and end apart: 3 -> 23, of which waited for: 2 -> 10; matrix products, arithmetic and copies ran while one was open for 15% -> 8% of each run, Pallas kernels for 0% -> 7%
where the time goes in v1:
time: 120 us
  waiting for transfers between devices  47.7 us (40%)
  starting transfers between devices  30.1 us (25%)
  Pallas kernels  26.2 us (22%)
  other arithmetic  10.2 us (8%)
  local copies, waits for them, and re-layouts  5.38 us (4%)
    ppermute x23, waiting for transfers between devices, send(): return lax.ppermute(value, AXES, pairs)  47.7 us
    ppermute x23, starting transfers between devices, send(): return lax.ppermute(value, AXES, pairs)  30.1 us
    pallas_call x5, Pallas kernels, score(): pl.pallas_call(functools.partial(score_kernel, sizes, len(chunks), bool(p...  22.8 us
    unnamed x26, local copies, waits for them, and re-layouts  5.09 us
    select_n x4, other arithmetic, for_x(): return jnp.where(odd, mine[k], two[k])  4.36 us
    pallas_call x1, Pallas kernels, gather(): pl.pallas_call(functools.partial(gather_kernel, share), out_shape=jax.Sha...  2.49 us
  transfers between devices with their start and end apart: 23, of which 10 were waited for; matrix products, arithmetic and copies ran while one was open for 8% of the time, Pallas kernels for 7%

profile of v1, /device:TPU:0, one launch (start us, length us, event | category | flops | bytes accessed | tf_op | source)
XLA Modules:
  0.0 119.8 jit_solution(8459570893792559576)
XLA Ops:
  0.5 2.2 %copy-done = bf16[2048,1024]{1,0:T(8,128)(2,1)S(1)} copy-done((bf16[2048,1024]{1,0:T(8,128)(2,1)S(1)}, bf16[2048,1024]{1,0:T(8,128)(2,1)}, u32[]{:S(2)}) %copy-start) | copy-done | bytes 4194328
  3.3 2.5 %shard_map.40 = bf16[32,1024]{1,0:T(8,128)(2,1)S(1)} custom-call(s32[128]{0:T(128)S(1)} %copy-done.10, bf16[2048,1024]{1,0:T(8,128)(2,1)S(1)} %copy-done), custom_call_target="tpu_custom_call" | custom-call | flops 33554432 | bytes 1048576 | tf_op jit(solution)/shard_map/pallas_call | solution.py:87
  5.9 2.5 %collective-permute-start.2 = (bf16[32,1024]{1,0:T(8,128)(2,1)S(1)}, bf16[32,1024]{1,0:T(8,128)(2,1)S(1)}, u32[]{:S(2)}, u32[]{:S(2)}) collective-permute-start(bf16[32,1024]{1,0:T(8,128)(2,1)S(1)} %shard_map.40), channel_id=1, source_target_pairs={{0,1},{1,0},{2,3},{3,2},{4,5},{5,4},{6,7},{7,6},{8,9},{9,8},{10,11... | collective-permute-start | bytes 196616 | tf_op jit(solution)/shard_map/ppermute | solution.py:195
  8.7 3.7 %collective-permute-start.7 = (bf16[192,1024]{1,0:T(8,128)(2,1)S(1)}, bf16[192,1024]{1,0:T(8,128)(2,1)}, u32[]{:S(2)}, u32[]{:S(2)}) collective-permute-start(bf16[192,1024]{1,0:T(8,128)(2,1)S(1)} %get-tuple-element.12.refs_1_.refs_2_), channel_id=1, source_target_pairs={{0,6},{1,7},{2,0},{3,1},{4,2},{5,3},{6,4},{7,5},{8,14},{9,15},{10,... | collective-permute-start | bytes 1179656 | tf_op jit(solution)/shard_map/ppermute | solution.py:195
  12.8 1.6 %collective-permute-start.3 = (bf16[32,1024]{1,0:T(8,128)(2,1)S(1)}, bf16[32,1024]{1,0:T(8,128)(2,1)S(1)}, u32[]{:S(2)}, u32[]{:S(2)}) collective-permute-start(bf16[32,1024]{1,0:T(8,128)(2,1)S(1)} %add.18), channel_id=1, source_target_pairs={{0,2},{1,3},{2,0},{3,1},{4,6},{5,7},{6,4},{7,5},{8,10},{9,11},{10,... | collective-permute-start | bytes 196616 | tf_op jit(solution)/shard_map/ppermute | solution.py:195
  14.9 13.9 %collective-permute-done.3 = bf16[32,1024]{1,0:T(8,128)(2,1)S(1)} collective-permute-done((bf16[32,1024]{1,0:T(8,128)(2,1)S(1)}, bf16[32,1024]{1,0:T(8,128)(2,1)S(1)}, u32[]{:S(2)}, u32[]{:S(2)}) %collective-permute-start.3) | collective-permute-done | bytes 65568 | tf_op jit(solution)/shard_map/ppermute | solution.py:195
  29.4 2.4 %collective-permute-start.4 = (bf16[32,1024]{1,0:T(8,128)(2,1)}, bf16[32,1024]{1,0:T(8,128)(2,1)}, u32[]{:S(2)}, u32[]{:S(2)}) collective-permute-start(bf16[32,1024]{1,0:T(8,128)(2,1)} %add.19), channel_id=1, source_target_pairs={{0,4},{1,5},{2,6},{3,7},{4,0},{5,1},{6,2},{7,3},{8,12},{9,13},{10,... | collective-permute-start | bytes 196616 | tf_op jit(solution)/shard_map/ppermute | solution.py:195
  33.3 1.7 %collective-permute-done.4 = bf16[32,1024]{1,0:T(8,128)(2,1)} collective-permute-done((bf16[32,1024]{1,0:T(8,128)(2,1)}, bf16[32,1024]{1,0:T(8,128)(2,1)}, u32[]{:S(2)}, u32[]{:S(2)}) %collective-permute-start.4) | collective-permute-done | bytes 65568 | tf_op jit(solution)/shard_map/ppermute | solution.py:195
  34.9 4.7 %collective-permute-start.10 = (bf16[176,1024]{1,0:T(8,128)(2,1)S(1)}, bf16[176,1024]{1,0:T(8,128)(2,1)S(1)}, u32[]{:S(2)}, u32[]{:S(2)}) collective-permute-start(bf16[176,1024]{1,0:T(8,128)(2,1)S(1)} %get-tuple-element.13.refs_2_.refs_3_), channel_id=1, source_target_pairs={{0,6},{1,7},{2,0},{3,1},{4,2},{5,3},{6,4},{7,5},{8,14},{9,15},{10,... | collective-permute-start | bytes 1081352 | tf_op jit(solution)/shard_map/ppermute | solution.py:195
  41.7 1.7 %broadcast_select_fusion.3 = bf16[144,1024]{1,0:T(8,128)(2,1)} fusion(bf16[144,1024]{1,0:T(8,128)(2,1)S(1)} %get-tuple-element.11.refs_0_.refs_1_, bf16[144,1024]{1,0:T(8,128)(2,1)} %collective-permute-done.6.refs_0_, pred[]{:T(512)S(6)} %eq.20), kind=kLoop, calls=%fused_computation.5 | loop fusion | flops 147456 | bytes 884737 | tf_op jit(solution)/shard_map/jit(_where)/select_n | solution.py:239
  43.4 11.5 %collective-permute-done.11.refs_3_ = bf16[176,1024]{1,0:T(8,128)(2,1)S(1)} collective-permute-done((bf16[176,1024]{1,0:T(8,128)(2,1)S(1)}, bf16[176,1024]{1,0:T(8,128)(2,1)S(1)}, u32[]{:S(2)}, u32[]{:S(2)}) %collective-permute-start.11) | collective-permute-done | bytes 360480 | tf_op jit(solution)/shard_map/ppermute | solution.py:195
  56.3 1.6 %collective-permute-start.18 = (bf16[192,1024]{1,0:T(8,128)(2,1)}, bf16[192,1024]{1,0:T(8,128)(2,1)}, u32[]{:S(2)}, u32[]{:S(2)}) collective-permute-start(bf16[192,1024]{1,0:T(8,128)(2,1)} %collective-permute-done.13.refs_5_), channel_id=1, source_target_pairs={{0,16},{1,17},{2,18},{3,19},{4,20},{5,21},{6,22},{7,23},{8,24},{9,... | collective-permute-start | bytes 1179656 | tf_op jit(solution)/shard_map/ppermute | solution.py:195
  63.7 2.5 %collective-permute-start.17 = (bf16[144,1024]{1,0:T(8,128)(2,1)}, bf16[144,1024]{1,0:T(8,128)(2,1)S(1)}, u32[]{:S(2)}, u32[]{:S(2)}) collective-permute-start(bf16[144,1024]{1,0:T(8,128)(2,1)} %collective-permute-done.12.refs_4_), channel_id=1, source_target_pairs={{0,16},{1,17},{2,18},{3,19},{4,20},{5,21},{6,22},{7,23},{8,24},{9,... | collective-permute-start | bytes 884744 | tf_op jit(solution)/shard_map/ppermute | solution.py:195
  67.2 4.3 %collective-permute-done.16.refs_1_ = bf16[176,1024]{1,0:T(8,128)(2,1)} collective-permute-done((bf16[176,1024]{1,0:T(8,128)(2,1)}, bf16[176,1024]{1,0:T(8,128)(2,1)}, u32[]{:S(2)}, u32[]{:S(2)}) %collective-permute-start.16) | collective-permute-done | bytes 360480 | tf_op jit(solution)/shard_map/ppermute | solution.py:195
  71.5 2.5 %collective-permute-start.8 = (bf16[144,1024]{1,0:T(8,128)(2,1)}, bf16[144,1024]{1,0:T(8,128)(2,1)S(1)}, u32[]{:S(2)}, u32[]{:S(2)}) collective-permute-start(bf16[144,1024]{1,0:T(8,128)(2,1)} %collective-permute-done.6.refs_0_), channel_id=1, source_target_pairs={{0,16},{1,17},{2,18},{3,19},{4,20},{5,21},{6,22},{7,23},{8,24},{9,... | collective-permute-start | bytes 884744 | tf_op jit(solution)/shard_map/ppermute | solution.py:195
  74.0 4.6 %collective-permute-done.15.refs_0_ = bf16[176,1024]{1,0:T(8,128)(2,1)} collective-permute-done((bf16[176,1024]{1,0:T(8,128)(2,1)}, bf16[176,1024]{1,0:T(8,128)(2,1)}, u32[]{:S(2)}, u32[]{:S(2)}) %collective-permute-start.15) | collective-permute-done | bytes 360480 | tf_op jit(solution)/shard_map/ppermute | solution.py:195
  80.1 4.7 %shard_map.44 = f32[1,768]{1,0:T(1,128)S(1)} custom-call(bf16[176,1024]{1,0:T(8,128)(2,1)} %collective-permute-done.15.refs_0_, bf16[176,1024]{1,0:T(8,128)(2,1)} %collective-permute-done.16.refs_1_, bf16[144,1024]{1,0:T(8,128)(2,1)S(1)} %collective-permute-done.17.refs_2_, bf16[192,1024]{1,0:T(8,128)(2,1)} %collective-permute-done.18.refs_3_, ...), custom_call_target="tpu_custom_call" | custom-call | flops 2885681152 | bytes 5603328 | tf_op jit(solution)/shard_map/pallas_call | solution.py:160
  85.0 4.3 %collective-permute-done.9.refs_1_ = bf16[192,1024]{1,0:T(8,128)(2,1)S(1)} collective-permute-done((bf16[192,1024]{1,0:T(8,128)(2,1)}, bf16[192,1024]{1,0:T(8,128)(2,1)S(1)}, u32[]{:S(2)}, u32[]{:S(2)}) %collective-permute-start.9) | collective-permute-done | bytes 393248 | tf_op jit(solution)/shard_map/ppermute | solution.py:195
  89.3 6.5 %shard_map.43 = f32[1,1024]{1,0:T(1,128)S(1)} custom-call(bf16[144,1024]{1,0:T(8,128)(2,1)S(1)} %collective-permute-done.8.refs_0_, bf16[192,1024]{1,0:T(8,128)(2,1)S(1)} %collective-permute-done.9.refs_1_, bf16[176,1024]{1,0:T(8,128)(2,1)S(1)} %copy-done.7, bf16[176,1024]{1,0:T(8,128)(2,1)S(1)} %copy-done.9, ...), custom_call_target="tpu_custom_call" | custom-call | flops 4294967296 | bytes 6291456 | tf_op jit(solution)/shard_map/pallas_call | solution.py:160
  95.9 4.0 %shard_map.39 = f32[1,768]{1,0:T(1,128)S(1)} custom-call(bf16[144,1024]{1,0:T(8,128)(2,1)S(1)} %get-tuple-element.11.refs_0_.refs_1_, bf16[192,1024]{1,0:T(8,128)(2,1)S(1)} %get-tuple-element.12.refs_1_.refs_2_, bf16[176,1024]{1,0:T(8,128)(2,1)S(1)} %get-tuple-element.13.refs_2_.refs_3_, bf16[176,1024]{1,0:T(8,128)(2,1)S(1)} %get-tuple-element.14.refs_3_.refs_4_, ...), custom_call_target="tpu_custom_call" | custom-call | flops 2885681152 | bytes 5603328 | tf_op jit(solution)/shard_map/pallas_call | solution.py:160
  99.9 4.4 %shard_map.41 = f32[1,1024]{1,0:T(1,128)S(1)} custom-call(bf16[336,1024]{1,0:T(8,128)(2,1)S(1)} %copy-done.5, bf16[144,1024]{1,0:T(8,128)(2,1)S(1)} %get-tuple-element.11.refs_0_.refs_1_, bf16[192,1024]{1,0:T(8,128)(2,1)S(1)} %get-tuple-element.12.refs_1_.refs_2_, bf16[176,1024]{1,0:T(8,128)(2,1)S(1)} %get-tuple-element.13.refs_2_.refs_3_, ...), custom_call_target="tpu_custom_call" | custom-call | flops 1409286144 | bytes 6291456 | tf_op jit(solution)/shard_map/pallas_call | solution.py:160
  104.5 3.2 %shard_map.42 = f32[1,384]{1,0:T(1,128)S(1)} custom-call(bf16[144,1024]{1,0:T(8,128)(2,1)} %collective-permute-done.6.refs_0_, bf16[192,1024]{1,0:T(8,128)(2,1)} %collective-permute-done.7.refs_1_, bf16[1024,1024]{1,0:T(8,128)(2,1)S(1)} %copy-done.3, bf16[1024,1024]{1,0:T(8,128)(2,1)} %collective-permute-done.refs_5_.refs_6_.refs_3_.refs_7_, ...), custom_call_target="tpu_custom_call" | custom-call | flops 1409286144 | bytes 4882432 | tf_op jit(solution)/shard_map/pallas_call | solution.py:160
  109.3 5.2 %collective-permute-done.19 = f32[1024]{0:T(1024)S(1)} collective-permute-done((f32[1024]{0:T(1024)S(1)}, f32[1024]{0:T(1024)S(1)}, u32[]{:S(2)}, u32[]{:S(2)}) %collective-permute-start.19) | collective-permute-done | bytes 4128 | tf_op jit(solution)/shard_map/ppermute | solution.py:195
  114.6 1.5 %collective-permute-start.20 = (f32[1024]{0:T(1024)S(1)}, f32[1024]{0:T(1024)S(1)}, u32[]{:S(2)}, u32[]{:S(2)}) collective-permute-start(f32[1024]{0:T(1024)S(1)} %fusion.2), channel_id=1, source_target_pairs={{0,16},{1,17},{2,18},{3,19},{4,20},{5,21},{6,22},{7,23},{8,24},{9,... | collective-permute-start | bytes 12296 | tf_op jit(solution)/shard_map/ppermute | solution.py:195
  (82 shorter events, 21.8 us)
Async XLA Ops:
  0.0 80.1 %collective-permute-start = (bf16[1024,1024]{1,0:T(8,128)(2,1)}, bf16[1024,1024]{1,0:T(8,128)(2,1)}, u32[]{:S(2)}, u32[]{:S(2)}) collective-permute-start(bf16[1024,1024]{1,0:T(8,128)(2,1)} %refs_4_.3), channel_id=1, source_target_pairs={{0,8},{1,9},{2,10},{3,11},{4,12},{5,13},{6,14},{7,15},{8,0},{9,1},... | collective-permute-start | bytes 6291464 | tf_op jit(solution)/shard_map/ppermute | solution.py:195
  5.8 26.0 %copy-start.1 = (bf16[2048,1024]{1,0:T(8,128)(2,1)S(1)}, bf16[2048,1024]{1,0:T(8,128)(2,1)}, u32[]{:S(2)}) copy-start(bf16[2048,1024]{1,0:T(8,128)(2,1)} %table.1) | copy-start | bytes 12582916
  5.9 6.9 %collective-permute-start.2 = (bf16[32,1024]{1,0:T(8,128)(2,1)S(1)}, bf16[32,1024]{1,0:T(8,128)(2,1)S(1)}, u32[]{:S(2)}, u32[]{:S(2)}) collective-permute-start(bf16[32,1024]{1,0:T(8,128)(2,1)S(1)} %shard_map.40), channel_id=1, source_target_pairs={{0,1},{1,0},{2,3},{3,2},{4,5},{5,4},{6,7},{7,6},{8,9},{9,8},{10,11... | collective-permute-start | bytes 196616 | tf_op jit(solution)/shard_map/ppermute | solution.py:195
  8.7 31.8 %collective-permute-start.7 = (bf16[192,1024]{1,0:T(8,128)(2,1)S(1)}, bf16[192,1024]{1,0:T(8,128)(2,1)}, u32[]{:S(2)}, u32[]{:S(2)}) collective-permute-start(bf16[192,1024]{1,0:T(8,128)(2,1)S(1)} %get-tuple-element.12.refs_1_.refs_2_), channel_id=1, source_target_pairs={{0,6},{1,7},{2,0},{3,1},{4,2},{5,3},{6,4},{7,5},{8,14},{9,15},{10,... | collective-permute-start | bytes 1179656 | tf_op jit(solution)/shard_map/ppermute | solution.py:195
  12.3 29.3 %collective-permute-start.6 = (bf16[144,1024]{1,0:T(8,128)(2,1)S(1)}, bf16[144,1024]{1,0:T(8,128)(2,1)}, u32[]{:S(2)}, u32[]{:S(2)}) collective-permute-start(bf16[144,1024]{1,0:T(8,128)(2,1)S(1)} %get-tuple-element.11.refs_0_.refs_1_), channel_id=1, source_target_pairs={{0,6},{1,7},{2,0},{3,1},{4,2},{5,3},{6,4},{7,5},{8,14},{9,15},{10,... | collective-permute-start | bytes 884744 | tf_op jit(solution)/shard_map/ppermute | solution.py:195
  12.8 16.0 %collective-permute-start.3 = (bf16[32,1024]{1,0:T(8,128)(2,1)S(1)}, bf16[32,1024]{1,0:T(8,128)(2,1)S(1)}, u32[]{:S(2)}, u32[]{:S(2)}) collective-permute-start(bf16[32,1024]{1,0:T(8,128)(2,1)S(1)} %add.18), channel_id=1, source_target_pairs={{0,2},{1,3},{2,0},{3,1},{4,6},{5,7},{6,4},{7,5},{8,10},{9,11},{10,... | collective-permute-start | bytes 196616 | tf_op jit(solution)/shard_map/ppermute | solution.py:195
  29.4 5.5 %collective-permute-start.4 = (bf16[32,1024]{1,0:T(8,128)(2,1)}, bf16[32,1024]{1,0:T(8,128)(2,1)}, u32[]{:S(2)}, u32[]{:S(2)}) collective-permute-start(bf16[32,1024]{1,0:T(8,128)(2,1)} %add.19), channel_id=1, source_target_pairs={{0,4},{1,5},{2,6},{3,7},{4,0},{5,1},{6,2},{7,3},{8,12},{9,13},{10,... | collective-permute-start | bytes 196616 | tf_op jit(solution)/shard_map/ppermute | solution.py:195
  31.8 27.6 %collective-permute-start.1 = (f32[1024]{0:T(1024)S(1)}, f32[1024]{0:T(1024)S(1)}, u32[]{:S(2)}, u32[]{:S(2)}) collective-permute-start(f32[1024]{0:T(1024)S(1)} %broadcast_multiply_fusion), channel_id=1, source_target_pairs={{0,8},{1,9},{2,10},{3,11},{4,12},{5,13},{6,14},{7,15},{8,0},{9,1},... | collective-permute-start | bytes 12296 | tf_op jit(solution)/shard_map/ppermute | solution.py:195
  34.9 21.4 %collective-permute-start.10 = (bf16[176,1024]{1,0:T(8,128)(2,1)S(1)}, bf16[176,1024]{1,0:T(8,128)(2,1)S(1)}, u32[]{:S(2)}, u32[]{:S(2)}) collective-permute-start(bf16[176,1024]{1,0:T(8,128)(2,1)S(1)} %get-tuple-element.13.refs_2_.refs_3_), channel_id=1, source_target_pairs={{0,6},{1,7},{2,0},{3,1},{4,2},{5,3},{6,4},{7,5},{8,14},{9,15},{10,... | collective-permute-start | bytes 1081352 | tf_op jit(solution)/shard_map/ppermute | solution.py:195
  40.5 14.4 %collective-permute-start.11 = (bf16[176,1024]{1,0:T(8,128)(2,1)S(1)}, bf16[176,1024]{1,0:T(8,128)(2,1)S(1)}, u32[]{:S(2)}, u32[]{:S(2)}) collective-permute-start(bf16[176,1024]{1,0:T(8,128)(2,1)S(1)} %get-tuple-element.14.refs_3_.refs_4_), channel_id=1, source_target_pairs={{0,6},{1,7},{2,0},{3,1},{4,2},{5,3},{6,4},{7,5},{8,14},{9,15},{10,... | collective-permute-start | bytes 1081352 | tf_op jit(solution)/shard_map/ppermute | solution.py:195
  41.6 14.7 %collective-permute-start.13 = (bf16[192,1024]{1,0:T(8,128)(2,1)S(1)}, bf16[192,1024]{1,0:T(8,128)(2,1)}, u32[]{:S(2)}, u32[]{:S(2)}) collective-permute-start(bf16[192,1024]{1,0:T(8,128)(2,1)S(1)} %broadcast_select_fusion), channel_id=1, source_target_pairs={{0,1},{1,0},{2,3},{3,2},{4,5},{5,4},{6,7},{7,6},{8,9},{9,8},{10,11... | collective-permute-start | bytes 1179656 | tf_op jit(solution)/shard_map/ppermute | solution.py:195
  55.0 8.8 %collective-permute-start.12 = (bf16[144,1024]{1,0:T(8,128)(2,1)}, bf16[144,1024]{1,0:T(8,128)(2,1)}, u32[]{:S(2)}, u32[]{:S(2)}) collective-permute-start(bf16[144,1024]{1,0:T(8,128)(2,1)} %broadcast_select_fusion.3), channel_id=1, source_target_pairs={{0,1},{1,0},{2,3},{3,2},{4,5},{5,4},{6,7},{7,6},{8,9},{9,8},{10,11... | collective-permute-start | bytes 884744 | tf_op jit(solution)/shard_map/ppermute | solution.py:195
  56.3 4.6 %collective-permute-start.5 = (bf16[32,1024]{1,0:T(8,128)(2,1)S(1)}, bf16[32,1024]{1,0:T(8,128)(2,1)S(1)}, u32[]{:S(2)}, u32[]{:S(2)}) collective-permute-start(bf16[32,1024]{1,0:T(8,128)(2,1)S(1)} %add.20), channel_id=1, source_target_pairs={{0,8},{1,9},{2,10},{3,11},{4,12},{5,13},{6,14},{7,15},{8,0},{9,1},... | collective-permute-start | bytes 196616 | tf_op jit(solution)/shard_map/ppermute | solution.py:195
  56.3 23.8 %collective-permute-start.18 = (bf16[192,1024]{1,0:T(8,128)(2,1)}, bf16[192,1024]{1,0:T(8,128)(2,1)}, u32[]{:S(2)}, u32[]{:S(2)}) collective-permute-start(bf16[192,1024]{1,0:T(8,128)(2,1)} %collective-permute-done.13.refs_5_), channel_id=1, source_target_pairs={{0,16},{1,17},{2,18},{3,19},{4,20},{5,21},{6,22},{7,23},{8,24},{9,... | collective-permute-start | bytes 1179656 | tf_op jit(solution)/shard_map/ppermute | solution.py:195
  59.4 12.0 %collective-permute-start.16 = (bf16[176,1024]{1,0:T(8,128)(2,1)}, bf16[176,1024]{1,0:T(8,128)(2,1)}, u32[]{:S(2)}, u32[]{:S(2)}) collective-permute-start(bf16[176,1024]{1,0:T(8,128)(2,1)} %broadcast_select_fusion.1), channel_id=1, source_target_pairs={{0,1},{1,0},{2,3},{3,2},{4,5},{5,4},{6,7},{7,6},{8,9},{9,8},{10,11... | collective-permute-start | bytes 1081352 | tf_op jit(solution)/shard_map/ppermute | solution.py:195
  61.6 17.0 %collective-permute-start.15 = (bf16[176,1024]{1,0:T(8,128)(2,1)}, bf16[176,1024]{1,0:T(8,128)(2,1)}, u32[]{:S(2)}, u32[]{:S(2)}) collective-permute-start(bf16[176,1024]{1,0:T(8,128)(2,1)} %broadcast_select_fusion.2), channel_id=1, source_target_pairs={{0,1},{1,0},{2,3},{3,2},{4,5},{5,4},{6,7},{7,6},{8,9},{9,8},{10,11... | collective-permute-start | bytes 1081352 | tf_op jit(solution)/shard_map/ppermute | solution.py:195
  63.7 16.4 %collective-permute-start.17 = (bf16[144,1024]{1,0:T(8,128)(2,1)}, bf16[144,1024]{1,0:T(8,128)(2,1)S(1)}, u32[]{:S(2)}, u32[]{:S(2)}) collective-permute-start(bf16[144,1024]{1,0:T(8,128)(2,1)} %collective-permute-done.12.refs_4_), channel_id=1, source_target_pairs={{0,16},{1,17},{2,18},{3,19},{4,20},{5,21},{6,22},{7,23},{8,24},{9,... | collective-permute-start | bytes 884744 | tf_op jit(solution)/shard_map/ppermute | solution.py:195
  71.5 13.5 %collective-permute-start.8 = (bf16[144,1024]{1,0:T(8,128)(2,1)}, bf16[144,1024]{1,0:T(8,128)(2,1)S(1)}, u32[]{:S(2)}, u32[]{:S(2)}) collective-permute-start(bf16[144,1024]{1,0:T(8,128)(2,1)} %collective-permute-done.6.refs_0_), channel_id=1, source_target_pairs={{0,16},{1,17},{2,18},{3,19},{4,20},{5,21},{6,22},{7,23},{8,24},{9,... | collective-permute-start | bytes 884744 | tf_op jit(solution)/shard_map/ppermute | solution.py:195
  78.6 10.7 %collective-permute-start.9 = (bf16[192,1024]{1,0:T(8,128)(2,1)}, bf16[192,1024]{1,0:T(8,128)(2,1)S(1)}, u32[]{:S(2)}, u32[]{:S(2)}) collective-permute-start(bf16[192,1024]{1,0:T(8,128)(2,1)} %collective-permute-done.7.refs_1_), channel_id=1, source_target_pairs={{0,16},{1,17},{2,18},{3,19},{4,20},{5,21},{6,22},{7,23},{8,24},{9,... | collective-permute-start | bytes 1179656 | tf_op jit(solution)/shard_map/ppermute | solution.py:195
  107.8 6.8 %collective-permute-start.14 = (f32[1024]{0:T(1024)S(1)}, f32[1024]{0:T(1024)S(1)}, u32[]{:S(2)}, u32[]{:S(2)}) collective-permute-start(f32[1024]{0:T(1024)S(1)} %pad_maximum_fusion.1), channel_id=1, source_target_pairs={{0,2},{1,3},{2,4},{3,5},{4,6},{5,7},{6,0},{7,1},{8,10},{9,11},{10,... | collective-permute-start | bytes 12296 | tf_op jit(solution)/shard_map/ppermute | solution.py:195
  107.9 6.6 %collective-permute-start.19 = (f32[1024]{0:T(1024)S(1)}, f32[1024]{0:T(1024)S(1)}, u32[]{:S(2)}, u32[]{:S(2)}) collective-permute-start(f32[1024]{0:T(1024)S(1)} %pad_maximum_fusion.2), channel_id=1, source_target_pairs={{0,1},{1,2},{2,3},{3,4},{4,5},{5,6},{6,7},{7,0},{8,9},{9,10},{10,1... | collective-permute-start | bytes 12296 | tf_op jit(solution)/shard_map/ppermute | solution.py:195
  114.6 3.6 %collective-permute-start.20 = (f32[1024]{0:T(1024)S(1)}, f32[1024]{0:T(1024)S(1)}, u32[]{:S(2)}, u32[]{:S(2)}) collective-permute-start(f32[1024]{0:T(1024)S(1)} %fusion.2), channel_id=1, source_target_pairs={{0,16},{1,17},{2,18},{3,19},{4,20},{5,21},{6,22},{7,23},{8,24},{9,... | collective-permute-start | bytes 12296 | tf_op jit(solution)/shard_map/ppermute | solution.py:195
  116.1 2.1 %collective-permute-start.21 = (f32[1024]{0:T(1024)S(1)}, f32[1024]{0:T(1024)S(1)}, u32[]{:S(2)}, u32[]{:S(2)}) collective-permute-start(f32[1024]{0:T(1024)S(1)} %fusion.2), channel_id=1, source_target_pairs={{0,8},{1,9},{2,10},{3,11},{4,12},{5,13},{6,14},{7,15},{8,0},{9,1},... | collective-permute-start | bytes 12296 | tf_op jit(solution)/shard_map/ppermute | solution.py:195
  116.1 3.0 %collective-permute-start.22 = (f32[1024]{0:T(1024)S(1)}, f32[1024]{0:T(1024)S(1)}, u32[]{:S(2)}, u32[]{:S(2)}) collective-permute-start(f32[1024]{0:T(1024)S(1)} %fusion.2), channel_id=1, source_target_pairs={{0,24},{1,25},{2,26},{3,27},{4,28},{5,29},{6,30},{7,31},{8,16},{9,... | collective-permute-start | bytes 12296 | tf_op jit(solution)/shard_map/ppermute | solution.py:195
  (12 other events, 73.7 us)

commit v2 on v1

--- a/solution.py
+++ b/solution.py
@@ -15,6 +15,7 @@
 LANES = 128
 PACK = 16
 KERNEL_BYTES = 16 * 2**20
+PICKED_BYTES = 16 * 2**20
 
 
 ANY = pl.BlockSpec(memory_space=pl.ANY)
@@ -103,12 +104,9 @@
     )(picks, table)
 
 
-def score_kernel(sizes, lead, picked, *refs):
+def score_kernel(sizes, *refs):
     sources = refs[: len(sizes)]
-    refs = list(refs[len(sizes) :])
-    near, far, near_half, far_half = refs[:4]
-    extra = refs[4:6] if picked else ()
-    out, rows, beyond, best, sems = refs[-5:]
+    near, far, near_half, far_half, out, rows, beyond, best, sems = refs[len(sizes) :]
     copies = []
     at = 0
     for k, size in enumerate(sizes):
@@ -116,51 +114,45 @@
             pltpu.make_async_copy(sources[k], rows.at[pl.ds(at, size)], sems.at[k])
         )
         at += size
-    total, main = at, sum(sizes[:lead])
+    total = at
     other = pltpu.make_async_copy(far, beyond, sems.at[len(sizes)])
     for copy in copies:
         copy.start()
     other.start()
     best[...] = jnp.full_like(best, -jnp.inf)
 
-    def against(block, halves, tile, count):
-        for t in range(0, block.shape[0], tile):
+    def against(block, halves):
+        for t in range(0, block.shape[0], TILE):
             inner = lax.dot_general(
-                rows[0:count, :],
-                block[t : t + tile, :],
+                rows[...],
+                block[t : t + TILE, :],
                 (((1,), (1,)), ((), ())),
                 preferred_element_type=jnp.float32,
             )
-            gain = inner - halves[:, t : t + tile]
-            reach = min(tile, LANES)
-            top = gain[:, :reach]
-            for k in range(LANES, tile, LANES):
+            gain = inner - halves[:, t : t + TILE]
+            top = gain[:, :LANES]
+            for k in range(LANES, TILE, LANES):
                 top = jnp.maximum(top, gain[:, k : k + LANES])
-            best[0:count, 0:reach] = jnp.maximum(best[0:count, 0:reach], top)
-
-    for copy in copies[:lead]:
+            best[0:total, :] = jnp.maximum(best[0:total, :], top)
+
+    for copy in copies:
         copy.wait()
-    against(near, near_half, TILE, main)
+    against(near, near_half)
     other.wait()
-    against(beyond, far_half, TILE, main)
-    for copy in copies[lead:]:
-        copy.wait()
-    if picked:
-        against(extra[0], extra[1], extra[0].shape[0], total)
+    against(beyond, far_half)
     out[...] = jnp.max(best[...].T, axis=0, keepdims=True)
 
 
-def score(chunks, near, far, near_half, far_half, only=(), picked=()):
-    sizes = [chunk.shape[0] for chunk in (*chunks, *only)]
-    main = sum(chunk.shape[0] for chunk in chunks)
+def score(chunks, near, far, near_half, far_half):
+    sizes = [chunk.shape[0] for chunk in chunks]
     total = sum(sizes)
     padded = -(-total // LANES) * LANES
     width = near.shape[1]
     block = near.shape[0]
     out = pl.pallas_call(
-        functools.partial(score_kernel, sizes, len(chunks), bool(picked)),
+        functools.partial(score_kernel, sizes),
         out_shape=jax.ShapeDtypeStruct((1, padded), jnp.float32),
-        in_specs=[ANY] * len(sizes) + [VMEM, ANY, VMEM, VMEM] + [VMEM] * len(picked),
+        in_specs=[ANY] * len(sizes) + [VMEM, ANY, VMEM, VMEM],
         out_specs=VMEM,
         scratch_shapes=[
             pltpu.VMEM((total, width), jnp.bfloat16),
@@ -169,12 +161,63 @@
             pltpu.SemaphoreType.DMA((len(sizes) + 1,)),
         ],
         cost_estimate=pl.CostEstimate(
-            flops=4 * main * block * width,
+            flops=4 * total * block * width,
             bytes_accessed=2 * width * (total + 2 * block),
             transcendentals=0,
         ),
         compiler_params=pltpu.CompilerParams(vmem_limit_bytes=KERNEL_BYTES),
-    )(*chunks, *only, near, far, near_half, far_half, *picked)
+    )(*chunks, near, far, near_half, far_half)
+    return out[0]
+
+
+def picked_kernel(sizes, *refs):
+    sources = refs[: len(sizes)]
+    chosen, out, rows, best, sems = refs[len(sizes) :]
+    copies = []
+    at = 0
+    for k, size in enumerate(sizes):
+        copies.append(
+            pltpu.make_async_copy(sources[k], rows.at[pl.ds(at, size)], sems.at[k])
+        )
+        at += size
+    for copy in copies:
+        copy.start()
+    best[...] = jnp.full_like(best, -jnp.inf)
+    wide = chosen[...].astype(jnp.float32)
+    half = 0.5 * jnp.sum((wide * wide).T, axis=0, keepdims=True)
+    for copy in copies:
+        copy.wait()
+    inner = lax.dot_general(
+        rows[...],
+        chosen[...],
+        (((1,), (1,)), ((), ())),
+        preferred_element_type=jnp.float32,
+    )
+    best[:, 0 : chosen.shape[0]] = inner - half
+    out[...] = jnp.max(best[...].T, axis=0, keepdims=True)
+
+
+def score_picked(chunks, chosen):
+    sizes = [chunk.shape[0] for chunk in chunks]
+    total = sum(sizes)
+    count, width = chosen.shape
+    out = pl.pallas_call(
+        functools.partial(picked_kernel, sizes),
+        out_shape=jax.ShapeDtypeStruct((1, total), jnp.float32),
+        in_specs=[ANY] * len(sizes) + [VMEM],
+        out_specs=VMEM,
+        scratch_shapes=[
+            pltpu.VMEM((total, width), jnp.bfloat16),
+            pltpu.VMEM((total, LANES), jnp.float32),
+            pltpu.SemaphoreType.DMA((len(sizes),)),
+        ],
+        cost_estimate=pl.CostEstimate(
+            flops=2 * total * count * width,
+            bytes_accessed=2 * width * (total + count),
+            transcendentals=0,
+        ),
+        compiler_params=pltpu.CompilerParams(vmem_limit_bytes=PICKED_BYTES),
+    )(*chunks, chosen)
     return out[0]
 
 
@@ -232,8 +275,8 @@
     far_half = send(near_half, swap_core)[None, :]
     near_half = near_half[None, :]
 
-    def best(chunks, *more):
-        return score(chunks, labeled, far, near_half, far_half, *more)
+    def best(chunks):
+        return score(chunks, labeled, far, near_half, far_half)
 
     def for_x(k):
         return jnp.where(odd, mine[k], two[k])
@@ -243,6 +286,7 @@
     one_side = [send(one[k], swap_side) for k in range(2)]
 
     own_a = best(mine)
+    own_c = best([beyond])
     z_edge = best(two[:2])
     mid = best(two_side + two[2:] + one[:2])
     x_rest = best(one[2:] + one_side)
@@ -253,8 +297,7 @@
         chosen = chosen + send(chosen, lambda g, b: (g, b ^ hop))
         hop *= 2
     chosen = jnp.concatenate([chosen, send(chosen, swap_core)])
-    chosen_half = 0.5 * squares(chosen)[None, :]
-    own_b = best([beyond], mine, (chosen, chosen_half))
+    picked = score_picked(mine + [beyond], chosen)
 
     def ordered(near, between, beyond):
         lower = jnp.where(side == 0, near, beyond)
@@ -264,8 +307,9 @@
     two_all = ordered(z_edge[:edge], mid[edge : edge + middle], mid[:edge])
     from_two = send(two_all, ahead_two)
     mid_later, _ = lax.optimization_barrier((mid, two_all))
-    own_near = jnp.maximum(own_a[: edge + middle], own_b[edge:half])
-    own_all = ordered(own_near[:edge], own_near[edge:], own_b[:edge])
+    own_near = jnp.concatenate([own_a[: edge + middle], own_c[:edge]])
+    own_near = jnp.maximum(own_near, picked)
+    own_all = ordered(own_near[:edge], own_near[edge:-edge], own_near[-edge:])
     at = edge + middle
     one_all = ordered(
         mid_later[at : at + edge], x_rest[:middle], x_rest[middle : middle + edge]

time: 120 us -> 117 us (0.975)
  waiting for transfers between devices: 47.7 us -> 53 us
  starting transfers between devices: 30.1 us -> 25.8 us
  other arithmetic: 10.2 us -> 7.11 us
    ppermute x23, waiting for transfers between devices: 47.7 us -> 53 us  [send(): return lax.ppermute(value, AXES, pairs)]
    ppermute x23, starting transfers between devices: 30.1 us -> 25.8 us  [send(): return lax.ppermute(value, AXES, pairs)]
    select_n x4, other arithmetic: 4.36 us -> 3.1 us  [for_x(): return jnp.where(odd, mine[k], two[k])]
    pallas_call x5 -> x6, Pallas kernels: 22.8 us -> 22.1 us  [the longest x5 20.1 us: score(): pl.pallas_call(functools.partial(score_kernel, sizes), out_shape=jax.Shap...]
    unnamed x26 -> x12, local copies, waits for them, and re-layouts: 5.09 us -> 4.8 us
  transfers between devices with their start and end apart: 23 -> 23, of which waited for: 10 -> 12; matrix products, arithmetic and copies ran while one was open for 8% -> 6% of each run, Pallas kernels for 7% -> 14%
where the time goes in v2:
time: 117 us
  waiting for transfers between devices  53 us (45%)
  starting transfers between devices  25.8 us (22%)
  Pallas kernels  25.4 us (22%)
  other arithmetic  7.11 us (6%)
  local copies, waits for them, and re-layouts  5.1 us (4%)
    ppermute x23, waiting for transfers between devices, send(): return lax.ppermute(value, AXES, pairs)  53 us
    ppermute x23, starting transfers between devices, send(): return lax.ppermute(value, AXES, pairs)  25.8 us
    pallas_call x5, Pallas kernels, score(): pl.pallas_call(functools.partial(score_kernel, sizes), out_shape=jax.Shap...  20.1 us
    unnamed x12, local copies, waits for them, and re-layouts  4.8 us
    select_n x4, other arithmetic, for_x(): return jnp.where(odd, mine[k], two[k])  3.1 us
    pallas_call x1, Pallas kernels, gather(): pl.pallas_call(functools.partial(gather_kernel, share), out_shape=jax.Sha...  2.49 us
  transfers between devices with their start and end apart: 23, of which 12 were waited for; matrix products, arithmetic and copies ran while one was open for 6% of the time, Pallas kernels for 14%

profile of v2, /device:TPU:0, one launch (start us, length us, event | category | flops | bytes accessed | tf_op | source)
XLA Modules:
  0.0 116.7 jit_solution(10389418166280259555)
XLA Ops:
  0.5 2.2 %copy-done = bf16[2048,1024]{1,0:T(8,128)(2,1)S(1)} copy-done((bf16[2048,1024]{1,0:T(8,128)(2,1)S(1)}, bf16[2048,1024]{1,0:T(8,128)(2,1)}, u32[]{:S(2)}) %copy-start) | copy-done | bytes 4194328
  3.3 2.5 %shard_map.41 = bf16[32,1024]{1,0:T(8,128)(2,1)S(1)} custom-call(s32[128]{0:T(128)S(1)} %copy-done.5, bf16[2048,1024]{1,0:T(8,128)(2,1)S(1)} %copy-done), custom_call_target="tpu_custom_call" | custom-call | flops 33554432 | bytes 1048576 | tf_op jit(solution)/shard_map/pallas_call | solution.py:88
  5.8 2.5 %collective-permute-start.2 = (bf16[32,1024]{1,0:T(8,128)(2,1)S(1)}, bf16[32,1024]{1,0:T(8,128)(2,1)S(1)}, u32[]{:S(2)}, u32[]{:S(2)}) collective-permute-start(bf16[32,1024]{1,0:T(8,128)(2,1)S(1)} %shard_map.41), channel_id=1, source_target_pairs={{0,1},{1,0},{2,3},{3,2},{4,5},{5,4},{6,7},{7,6},{8,9},{9,8},{10,11... | collective-permute-start | bytes 196616 | tf_op jit(solution)/shard_map/ppermute | solution.py:238
  8.4 2.8 %collective-permute-done.2 = bf16[32,1024]{1,0:T(8,128)(2,1)S(1)} collective-permute-done((bf16[32,1024]{1,0:T(8,128)(2,1)S(1)}, bf16[32,1024]{1,0:T(8,128)(2,1)S(1)}, u32[]{:S(2)}, u32[]{:S(2)}) %collective-permute-start.2) | collective-permute-done | bytes 65568 | tf_op jit(solution)/shard_map/ppermute | solution.py:238
  11.2 1.9 %collective-permute-start.3 = (bf16[32,1024]{1,0:T(8,128)(2,1)S(1)}, bf16[32,1024]{1,0:T(8,128)(2,1)S(1)}, u32[]{:S(2)}, u32[]{:S(2)}) collective-permute-start(bf16[32,1024]{1,0:T(8,128)(2,1)S(1)} %add.18), channel_id=1, source_target_pairs={{0,2},{1,3},{2,0},{3,1},{4,6},{5,7},{6,4},{7,5},{8,10},{9,11},{10,... | collective-permute-start | bytes 196616 | tf_op jit(solution)/shard_map/ppermute | solution.py:238
  13.3 2.5 %collective-permute-start.7 = (bf16[192,1024]{1,0:T(8,128)(2,1)S(1)}, bf16[192,1024]{1,0:T(8,128)(2,1)}, u32[]{:S(2)}, u32[]{:S(2)}) collective-permute-start(bf16[192,1024]{1,0:T(8,128)(2,1)S(1)} %get-tuple-element.12.refs_1_), channel_id=1, source_target_pairs={{0,6},{1,7},{2,0},{3,1},{4,2},{5,3},{6,4},{7,5},{8,14},{9,15},{10,... | collective-permute-start | bytes 1179656 | tf_op jit(solution)/shard_map/ppermute | solution.py:238
  19.0 1.9 %collective-permute-start.4 = (bf16[32,1024]{1,0:T(8,128)(2,1)S(1)}, bf16[32,1024]{1,0:T(8,128)(2,1)S(1)}, u32[]{:S(2)}, u32[]{:S(2)}) collective-permute-start(bf16[32,1024]{1,0:T(8,128)(2,1)S(1)} %add.19), channel_id=1, source_target_pairs={{0,4},{1,5},{2,6},{3,7},{4,0},{5,1},{6,2},{7,3},{8,12},{9,13},{10,... | collective-permute-start | bytes 196616 | tf_op jit(solution)/shard_map/ppermute | solution.py:238
  21.4 19.4 %collective-permute-done.4 = bf16[32,1024]{1,0:T(8,128)(2,1)S(1)} collective-permute-done((bf16[32,1024]{1,0:T(8,128)(2,1)S(1)}, bf16[32,1024]{1,0:T(8,128)(2,1)S(1)}, u32[]{:S(2)}, u32[]{:S(2)}) %collective-permute-start.4) | collective-permute-done | bytes 65568 | tf_op jit(solution)/shard_map/ppermute | solution.py:238
  41.4 1.6 %collective-permute-done.5 = bf16[32,1024]{1,0:T(8,128)(2,1)} collective-permute-done((bf16[32,1024]{1,0:T(8,128)(2,1)}, bf16[32,1024]{1,0:T(8,128)(2,1)}, u32[]{:S(2)}, u32[]{:S(2)}) %collective-permute-start.5) | collective-permute-done | bytes 65568 | tf_op jit(solution)/shard_map/ppermute | solution.py:238
  43.0 4.1 %collective-permute-start.11 = (bf16[176,1024]{1,0:T(8,128)(2,1)S(1)}, bf16[176,1024]{1,0:T(8,128)(2,1)S(1)}, u32[]{:S(2)}, u32[]{:S(2)}) collective-permute-start(bf16[176,1024]{1,0:T(8,128)(2,1)S(1)} %get-tuple-element.14.refs_3_), channel_id=1, source_target_pairs={{0,6},{1,7},{2,0},{3,1},{4,2},{5,3},{6,4},{7,5},{8,14},{9,15},{10,... | collective-permute-start | bytes 1081352 | tf_op jit(solution)/shard_map/ppermute | solution.py:238
  49.1 1.9 %shard_map.42 = f32[1,1024]{1,0:T(1,128)S(1)} custom-call(bf16[144,1024]{1,0:T(8,128)(2,1)S(1)} %get-tuple-element.11.refs_0_, bf16[192,1024]{1,0:T(8,128)(2,1)S(1)} %get-tuple-element.12.refs_1_, bf16[176,1024]{1,0:T(8,128)(2,1)S(1)} %get-tuple-element.13.refs_2_, bf16[176,1024]{1,0:T(8,128)(2,1)S(1)} %get-tuple-element.14.refs_3_, ...), custom_call_target="tpu_custom_call" | custom-call | flops 134217728 | bytes 2228224 | tf_op jit(solution)/shard_map/pallas_call | solution.py:204
  56.7 1.6 %collective-permute-start.8 = (bf16[144,1024]{1,0:T(8,128)(2,1)}, bf16[144,1024]{1,0:T(8,128)(2,1)S(1)}, u32[]{:S(2)}, u32[]{:S(2)}) collective-permute-start(bf16[144,1024]{1,0:T(8,128)(2,1)} %collective-permute-done.6.refs_0_), channel_id=1, source_target_pairs={{0,16},{1,17},{2,18},{3,19},{4,20},{5,21},{6,22},{7,23},{8,24},{9,... | collective-permute-start | bytes 884744 | tf_op jit(solution)/shard_map/ppermute | solution.py:238
  59.4 2.7 %collective-permute-done.12.refs_4_ = bf16[144,1024]{1,0:T(8,128)(2,1)S(1)} collective-permute-done((bf16[144,1024]{1,0:T(8,128)(2,1)S(1)}, bf16[144,1024]{1,0:T(8,128)(2,1)S(1)}, u32[]{:S(2)}, u32[]{:S(2)}) %collective-permute-start.12) | collective-permute-done | bytes 294944 | tf_op jit(solution)/shard_map/ppermute | solution.py:238
  62.7 7.9 %collective-permute-done.13.refs_5_ = bf16[192,1024]{1,0:T(8,128)(2,1)S(1)} collective-permute-done((bf16[192,1024]{1,0:T(8,128)(2,1)S(1)}, bf16[192,1024]{1,0:T(8,128)(2,1)S(1)}, u32[]{:S(2)}, u32[]{:S(2)}) %collective-permute-start.13) | collective-permute-done | bytes 393248 | tf_op jit(solution)/shard_map/ppermute | solution.py:238
  72.6 2.9 %shard_map.40 = f32[1,384]{1,0:T(1,128)S(1)} custom-call(bf16[336,1024]{1,0:T(8,128)(2,1)S(1)} %copy-done.4, bf16[1024,1024]{1,0:T(8,128)(2,1)S(1)} %copy-done.2, bf16[1024,1024]{1,0:T(8,128)(2,1)} %collective-permute-done.refs_5_.refs_2_.refs_3_.refs_7_, f32[1,1024]{1,0:T(1,128)S(1)} %bitcast.6, f32[1,1024]{1,0:T(1,128)S(1)} %bitcast.11), custom_call_target="tpu_custom_call" | custom-call | flops 1409286144 | bytes 4882432 | tf_op jit(solution)/shard_map/pallas_call | solution.py:152
  75.4 4.0 %shard_map.39 = f32[1,768]{1,0:T(1,128)S(1)} custom-call(bf16[144,1024]{1,0:T(8,128)(2,1)S(1)} %get-tuple-element.11.refs_0_, bf16[192,1024]{1,0:T(8,128)(2,1)S(1)} %get-tuple-element.12.refs_1_, bf16[176,1024]{1,0:T(8,128)(2,1)S(1)} %get-tuple-element.13.refs_2_, bf16[176,1024]{1,0:T(8,128)(2,1)S(1)} %get-tuple-element.14.refs_3_, ...), custom_call_target="tpu_custom_call" | custom-call | flops 2885681152 | bytes 5603328 | tf_op jit(solution)/shard_map/pallas_call | solution.py:152
  79.5 1.6 %collective-permute-start.9 = (bf16[192,1024]{1,0:T(8,128)(2,1)}, bf16[192,1024]{1,0:T(8,128)(2,1)S(1)}, u32[]{:S(2)}, u32[]{:S(2)}) collective-permute-start(bf16[192,1024]{1,0:T(8,128)(2,1)} %collective-permute-done.7.refs_1_), channel_id=1, source_target_pairs={{0,16},{1,17},{2,18},{3,19},{4,20},{5,21},{6,22},{7,23},{8,24},{9,... | collective-permute-start | bytes 1179656 | tf_op jit(solution)/shard_map/ppermute | solution.py:238
  81.0 4.5 %collective-permute-done.15.refs_0_ = bf16[176,1024]{1,0:T(8,128)(2,1)S(1)} collective-permute-done((bf16[176,1024]{1,0:T(8,128)(2,1)S(1)}, bf16[176,1024]{1,0:T(8,128)(2,1)S(1)}, u32[]{:S(2)}, u32[]{:S(2)}) %collective-permute-start.15) | collective-permute-done | bytes 360480 | tf_op jit(solution)/shard_map/ppermute | solution.py:238
  85.5 3.3 %collective-permute-done.18.refs_3_ = bf16[192,1024]{1,0:T(8,128)(2,1)S(1)} collective-permute-done((bf16[192,1024]{1,0:T(8,128)(2,1)S(1)}, bf16[192,1024]{1,0:T(8,128)(2,1)S(1)}, u32[]{:S(2)}, u32[]{:S(2)}) %collective-permute-start.18) | collective-permute-done | bytes 393248 | tf_op jit(solution)/shard_map/ppermute | solution.py:238
  88.8 4.0 %shard_map.45 = f32[1,768]{1,0:T(1,128)S(1)} custom-call(bf16[176,1024]{1,0:T(8,128)(2,1)S(1)} %collective-permute-done.15.refs_0_, bf16[176,1024]{1,0:T(8,128)(2,1)S(1)} %collective-permute-done.16.refs_1_, bf16[144,1024]{1,0:T(8,128)(2,1)S(1)} %collective-permute-done.17.refs_2_, bf16[192,1024]{1,0:T(8,128)(2,1)S(1)} %collective-permute-done.18.refs_3_, ...), custom_call_target="tpu_custom_call" | custom-call | flops 2885681152 | bytes 5603328 | tf_op jit(solution)/shard_map/pallas_call | solution.py:152
  93.0 2.4 %collective-permute-done.9.refs_1_ = bf16[192,1024]{1,0:T(8,128)(2,1)S(1)} collective-permute-done((bf16[192,1024]{1,0:T(8,128)(2,1)}, bf16[192,1024]{1,0:T(8,128)(2,1)S(1)}, u32[]{:S(2)}, u32[]{:S(2)}) %collective-permute-start.9) | collective-permute-done | bytes 393248 | tf_op jit(solution)/shard_map/ppermute | solution.py:238
  95.5 6.1 %shard_map.44 = f32[1,1024]{1,0:T(1,128)S(1)} custom-call(bf16[144,1024]{1,0:T(8,128)(2,1)S(1)} %collective-permute-done.8.refs_0_, bf16[192,1024]{1,0:T(8,128)(2,1)S(1)} %collective-permute-done.9.refs_1_, bf16[176,1024]{1,0:T(8,128)(2,1)} %collective-permute-done.10.refs_2_, bf16[176,1024]{1,0:T(8,128)(2,1)S(1)} %collective-permute-done.11.refs_3_, ...), custom_call_target="tpu_custom_call" | custom-call | flops 4294967296 | bytes 6291456 | tf_op jit(solution)/shard_map/pallas_call | solution.py:152
  101.7 3.2 %shard_map.43 = f32[1,384]{1,0:T(1,128)S(1)} custom-call(bf16[144,1024]{1,0:T(8,128)(2,1)} %collective-permute-done.6.refs_0_, bf16[192,1024]{1,0:T(8,128)(2,1)} %collective-permute-done.7.refs_1_, bf16[1024,1024]{1,0:T(8,128)(2,1)S(1)} %copy-done.2, bf16[1024,1024]{1,0:T(8,128)(2,1)} %collective-permute-done.refs_5_.refs_2_.refs_3_.refs_7_, ...), custom_call_target="tpu_custom_call" | custom-call | flops 1409286144 | bytes 4882432 | tf_op jit(solution)/shard_map/pallas_call | solution.py:152
  105.9 5.5 %collective-permute-done.19 = f32[1024]{0:T(1024)S(1)} collective-permute-done((f32[1024]{0:T(1024)S(1)}, f32[1024]{0:T(1024)S(1)}, u32[]{:S(2)}, u32[]{:S(2)}) %collective-permute-start.19) | collective-permute-done | bytes 4128 | tf_op jit(solution)/shard_map/ppermute | solution.py:238
  (69 shorter events, 23.4 us)
Async XLA Ops:
  0.0 72.1 %collective-permute-start = (bf16[1024,1024]{1,0:T(8,128)(2,1)}, bf16[1024,1024]{1,0:T(8,128)(2,1)}, u32[]{:S(2)}, u32[]{:S(2)}) collective-permute-start(bf16[1024,1024]{1,0:T(8,128)(2,1)} %refs_4_.3), channel_id=1, source_target_pairs={{0,8},{1,9},{2,10},{3,11},{4,12},{5,13},{6,14},{7,15},{8,0},{9,1},... | collective-permute-start | bytes 6291464 | tf_op jit(solution)/shard_map/ppermute | solution.py:238
  5.8 5.3 %collective-permute-start.2 = (bf16[32,1024]{1,0:T(8,128)(2,1)S(1)}, bf16[32,1024]{1,0:T(8,128)(2,1)S(1)}, u32[]{:S(2)}, u32[]{:S(2)}) collective-permute-start(bf16[32,1024]{1,0:T(8,128)(2,1)S(1)} %shard_map.41), channel_id=1, source_target_pairs={{0,1},{1,0},{2,3},{3,2},{4,5},{5,4},{6,7},{7,6},{8,9},{9,8},{10,11... | collective-permute-start | bytes 196616 | tf_op jit(solution)/shard_map/ppermute | solution.py:238
  11.2 7.8 %collective-permute-start.3 = (bf16[32,1024]{1,0:T(8,128)(2,1)S(1)}, bf16[32,1024]{1,0:T(8,128)(2,1)S(1)}, u32[]{:S(2)}, u32[]{:S(2)}) collective-permute-start(bf16[32,1024]{1,0:T(8,128)(2,1)S(1)} %add.18), channel_id=1, source_target_pairs={{0,2},{1,3},{2,0},{3,1},{4,6},{5,7},{6,4},{7,5},{8,10},{9,11},{10,... | collective-permute-start | bytes 196616 | tf_op jit(solution)/shard_map/ppermute | solution.py:238
  13.3 38.8 %collective-permute-start.7 = (bf16[192,1024]{1,0:T(8,128)(2,1)S(1)}, bf16[192,1024]{1,0:T(8,128)(2,1)}, u32[]{:S(2)}, u32[]{:S(2)}) collective-permute-start(bf16[192,1024]{1,0:T(8,128)(2,1)S(1)} %get-tuple-element.12.refs_1_), channel_id=1, source_target_pairs={{0,6},{1,7},{2,0},{3,1},{4,2},{5,3},{6,4},{7,5},{8,14},{9,15},{10,... | collective-permute-start | bytes 1179656 | tf_op jit(solution)/shard_map/ppermute | solution.py:238
  15.9 35.2 %collective-permute-start.6 = (bf16[144,1024]{1,0:T(8,128)(2,1)S(1)}, bf16[144,1024]{1,0:T(8,128)(2,1)}, u32[]{:S(2)}, u32[]{:S(2)}) collective-permute-start(bf16[144,1024]{1,0:T(8,128)(2,1)S(1)} %get-tuple-element.11.refs_0_), channel_id=1, source_target_pairs={{0,6},{1,7},{2,0},{3,1},{4,2},{5,3},{6,4},{7,5},{8,14},{9,15},{10,... | collective-permute-start | bytes 884744 | tf_op jit(solution)/shard_map/ppermute | solution.py:238
  18.9 37.8 %collective-permute-start.10 = (bf16[176,1024]{1,0:T(8,128)(2,1)S(1)}, bf16[176,1024]{1,0:T(8,128)(2,1)}, u32[]{:S(2)}, u32[]{:S(2)}) collective-permute-start(bf16[176,1024]{1,0:T(8,128)(2,1)S(1)} %get-tuple-element.13.refs_2_), channel_id=1, source_target_pairs={{0,6},{1,7},{2,0},{3,1},{4,2},{5,3},{6,4},{7,5},{8,14},{9,15},{10,... | collective-permute-start | bytes 1081352 | tf_op jit(solution)/shard_map/ppermute | solution.py:238
  19.0 21.8 %collective-permute-start.4 = (bf16[32,1024]{1,0:T(8,128)(2,1)S(1)}, bf16[32,1024]{1,0:T(8,128)(2,1)S(1)}, u32[]{:S(2)}, u32[]{:S(2)}) collective-permute-start(bf16[32,1024]{1,0:T(8,128)(2,1)S(1)} %add.19), channel_id=1, source_target_pairs={{0,4},{1,5},{2,6},{3,7},{4,0},{5,1},{6,2},{7,3},{8,12},{9,13},{10,... | collective-permute-start | bytes 196616 | tf_op jit(solution)/shard_map/ppermute | solution.py:238
  41.4 1.6 %collective-permute-start.5 = (bf16[32,1024]{1,0:T(8,128)(2,1)}, bf16[32,1024]{1,0:T(8,128)(2,1)}, u32[]{:S(2)}, u32[]{:S(2)}) collective-permute-start(bf16[32,1024]{1,0:T(8,128)(2,1)} %add.20), channel_id=1, source_target_pairs={{0,8},{1,9},{2,10},{3,11},{4,12},{5,13},{6,14},{7,15},{8,0},{9,1},... | collective-permute-start | bytes 196616 | tf_op jit(solution)/shard_map/ppermute | solution.py:238
  43.0 12.1 %collective-permute-start.11 = (bf16[176,1024]{1,0:T(8,128)(2,1)S(1)}, bf16[176,1024]{1,0:T(8,128)(2,1)S(1)}, u32[]{:S(2)}, u32[]{:S(2)}) collective-permute-start(bf16[176,1024]{1,0:T(8,128)(2,1)S(1)} %get-tuple-element.14.refs_3_), channel_id=1, source_target_pairs={{0,6},{1,7},{2,0},{3,1},{4,2},{5,3},{6,4},{7,5},{8,14},{9,15},{10,... | collective-permute-start | bytes 1081352 | tf_op jit(solution)/shard_map/ppermute | solution.py:238
  51.1 8.2 %collective-permute-start.1 = (f32[1024]{0:T(1024)S(1)}, f32[1024]{0:T(1024)S(1)}, u32[]{:S(2)}, u32[]{:S(2)}) collective-permute-start(f32[1024]{0:T(1024)S(1)} %broadcast_multiply_fusion), channel_id=1, source_target_pairs={{0,8},{1,9},{2,10},{3,11},{4,12},{5,13},{6,14},{7,15},{8,0},{9,1},... | collective-permute-start | bytes 12296 | tf_op jit(solution)/shard_map/ppermute | solution.py:238
  52.2 9.9 %collective-permute-start.12 = (bf16[144,1024]{1,0:T(8,128)(2,1)S(1)}, bf16[144,1024]{1,0:T(8,128)(2,1)S(1)}, u32[]{:S(2)}, u32[]{:S(2)}) collective-permute-start(bf16[144,1024]{1,0:T(8,128)(2,1)S(1)} %broadcast_select_fusion.3), channel_id=1, source_target_pairs={{0,1},{1,0},{2,3},{3,2},{4,5},{5,4},{6,7},{7,6},{8,9},{9,8},{10,11... | collective-permute-start | bytes 884744 | tf_op jit(solution)/shard_map/ppermute | solution.py:238
  55.1 15.4 %collective-permute-start.13 = (bf16[192,1024]{1,0:T(8,128)(2,1)S(1)}, bf16[192,1024]{1,0:T(8,128)(2,1)S(1)}, u32[]{:S(2)}, u32[]{:S(2)}) collective-permute-start(bf16[192,1024]{1,0:T(8,128)(2,1)S(1)} %broadcast_select_fusion), channel_id=1, source_target_pairs={{0,1},{1,0},{2,3},{3,2},{4,5},{5,4},{6,7},{7,6},{8,9},{9,8},{10,11... | collective-permute-start | bytes 1179656 | tf_op jit(solution)/shard_map/ppermute | solution.py:238
  56.7 36.3 %collective-permute-start.8 = (bf16[144,1024]{1,0:T(8,128)(2,1)}, bf16[144,1024]{1,0:T(8,128)(2,1)S(1)}, u32[]{:S(2)}, u32[]{:S(2)}) collective-permute-start(bf16[144,1024]{1,0:T(8,128)(2,1)} %collective-permute-done.6.refs_0_), channel_id=1, source_target_pairs={{0,16},{1,17},{2,18},{3,19},{4,20},{5,21},{6,22},{7,23},{8,24},{9,... | collective-permute-start | bytes 884744 | tf_op jit(solution)/shard_map/ppermute | solution.py:238
  59.3 20.1 %collective-permute-start.16 = (bf16[176,1024]{1,0:T(8,128)(2,1)S(1)}, bf16[176,1024]{1,0:T(8,128)(2,1)S(1)}, u32[]{:S(2)}, u32[]{:S(2)}) collective-permute-start(bf16[176,1024]{1,0:T(8,128)(2,1)S(1)} %broadcast_select_fusion.1), channel_id=1, source_target_pairs={{0,1},{1,0},{2,3},{3,2},{4,5},{5,4},{6,7},{7,6},{8,9},{9,8},{10,11... | collective-permute-start | bytes 1081352 | tf_op jit(solution)/shard_map/ppermute | solution.py:238
  62.1 23.4 %collective-permute-start.15 = (bf16[176,1024]{1,0:T(8,128)(2,1)S(1)}, bf16[176,1024]{1,0:T(8,128)(2,1)S(1)}, u32[]{:S(2)}, u32[]{:S(2)}) collective-permute-start(bf16[176,1024]{1,0:T(8,128)(2,1)S(1)} %broadcast_select_fusion.2), channel_id=1, source_target_pairs={{0,1},{1,0},{2,3},{3,2},{4,5},{5,4},{6,7},{7,6},{8,9},{9,8},{10,11... | collective-permute-start | bytes 1081352 | tf_op jit(solution)/shard_map/ppermute | solution.py:238
  70.5 15.0 %collective-permute-start.17 = (bf16[144,1024]{1,0:T(8,128)(2,1)S(1)}, bf16[144,1024]{1,0:T(8,128)(2,1)S(1)}, u32[]{:S(2)}, u32[]{:S(2)}) collective-permute-start(bf16[144,1024]{1,0:T(8,128)(2,1)S(1)} %collective-permute-done.12.refs_4_), channel_id=1, source_target_pairs={{0,16},{1,17},{2,18},{3,19},{4,20},{5,21},{6,22},{7,23},{8,24},{9,... | collective-permute-start | bytes 884744 | tf_op jit(solution)/shard_map/ppermute | solution.py:238
  72.1 16.8 %collective-permute-start.18 = (bf16[192,1024]{1,0:T(8,128)(2,1)S(1)}, bf16[192,1024]{1,0:T(8,128)(2,1)S(1)}, u32[]{:S(2)}, u32[]{:S(2)}) collective-permute-start(bf16[192,1024]{1,0:T(8,128)(2,1)S(1)} %collective-permute-done.13.refs_5_), channel_id=1, source_target_pairs={{0,16},{1,17},{2,18},{3,19},{4,20},{5,21},{6,22},{7,23},{8,24},{9,... | collective-permute-start | bytes 1179656 | tf_op jit(solution)/shard_map/ppermute | solution.py:238
  79.5 16.0 %collective-permute-start.9 = (bf16[192,1024]{1,0:T(8,128)(2,1)}, bf16[192,1024]{1,0:T(8,128)(2,1)S(1)}, u32[]{:S(2)}, u32[]{:S(2)}) collective-permute-start(bf16[192,1024]{1,0:T(8,128)(2,1)} %collective-permute-done.7.refs_1_), channel_id=1, source_target_pairs={{0,16},{1,17},{2,18},{3,19},{4,20},{5,21},{6,22},{7,23},{8,24},{9,... | collective-permute-start | bytes 1179656 | tf_op jit(solution)/shard_map/ppermute | solution.py:238
  101.6 12.1 %copy-start.1 = (bf16[2048,1024]{1,0:T(8,128)(2,1)S(1)}, bf16[2048,1024]{1,0:T(8,128)(2,1)}, u32[]{:S(2)}) copy-start(bf16[2048,1024]{1,0:T(8,128)(2,1)} %table.1) | copy-start | bytes 12582916
  105.0 6.5 %collective-permute-start.14 = (f32[1024]{0:T(1024)S(1)}, f32[1024]{0:T(1024)S(1)}, u32[]{:S(2)}, u32[]{:S(2)}) collective-permute-start(f32[1024]{0:T(1024)S(1)} %pad_maximum_fusion.1), channel_id=1, source_target_pairs={{0,2},{1,3},{2,4},{3,5},{4,6},{5,7},{6,0},{7,1},{8,10},{9,11},{10,... | collective-permute-start | bytes 12296 | tf_op jit(solution)/shard_map/ppermute | solution.py:238
  105.1 6.3 %collective-permute-start.19 = (f32[1024]{0:T(1024)S(1)}, f32[1024]{0:T(1024)S(1)}, u32[]{:S(2)}, u32[]{:S(2)}) collective-permute-start(f32[1024]{0:T(1024)S(1)} %pad_maximum_fusion.2), channel_id=1, source_target_pairs={{0,1},{1,2},{2,3},{3,4},{4,5},{5,6},{6,7},{7,0},{8,9},{9,10},{10,1... | collective-permute-start | bytes 12296 | tf_op jit(solution)/shard_map/ppermute | solution.py:238
  111.5 3.6 %collective-permute-start.20 = (f32[1024]{0:T(1024)S(1)}, f32[1024]{0:T(1024)S(1)}, u32[]{:S(2)}, u32[]{:S(2)}) collective-permute-start(f32[1024]{0:T(1024)S(1)} %fusion.2), channel_id=1, source_target_pairs={{0,16},{1,17},{2,18},{3,19},{4,20},{5,21},{6,22},{7,23},{8,24},{9,... | collective-permute-start | bytes 12296 | tf_op jit(solution)/shard_map/ppermute | solution.py:238
  113.0 2.1 %collective-permute-start.21 = (f32[1024]{0:T(1024)S(1)}, f32[1024]{0:T(1024)S(1)}, u32[]{:S(2)}, u32[]{:S(2)}) collective-permute-start(f32[1024]{0:T(1024)S(1)} %fusion.2), channel_id=1, source_target_pairs={{0,8},{1,9},{2,10},{3,11},{4,12},{5,13},{6,14},{7,15},{8,0},{9,1},... | collective-permute-start | bytes 12296 | tf_op jit(solution)/shard_map/ppermute | solution.py:238
  113.1 3.0 %collective-permute-start.22 = (f32[1024]{0:T(1024)S(1)}, f32[1024]{0:T(1024)S(1)}, u32[]{:S(2)}, u32[]{:S(2)}) collective-permute-start(f32[1024]{0:T(1024)S(1)} %fusion.2), channel_id=1, source_target_pairs={{0,24},{1,25},{2,26},{3,27},{4,28},{5,29},{6,30},{7,31},{8,16},{9,... | collective-permute-start | bytes 12296 | tf_op jit(solution)/shard_map/ppermute | solution.py:238
  (5 other events, 14.5 us)
